TPU v7x, 128 devices: a whole 4x4x4 slice. The times are simulated.
128 devices in a mesh: grp: 8 (over x, z_lo), wide: 16 (over y, z_hi, core).
Axes of the slice: x: 4, y: 4, z: 4 (z_hi: 2, z_lo: 2; z = z_hi * 2 + z_lo), core: 2. Of those that a mesh axis runs over, the one named last changes fastest.
Arguments:
- left_env: bfloat16 [64, 32, 128, 128], P('grp', 'wide'), may hold values from -0.5 to 0.5
- right_env: bfloat16 [128, 32, 128, 128], P('wide', 'grp'), may hold values from -0.09375 to 0.09375
- psi: bfloat16 [64, 128, 128, 128], P('grp', 'wide'), may hold values from -6 to 6
- left_shift: int32 [32], replicated, may hold values from -1 to 1
- right_shift: int32 [32], replicated, may hold values from -1 to 1
- active: int32 [64, 128, 32], P('grp', 'wide'), may hold values 0 or 1
Outputs:
- hpsi: float32 [64, 128, 128, 128], P('grp', 'wide')
All inputs are finite; a program needn't handle non-finite values. No bound on the sum of `active` on one device may be relied on, other than what follows from the above.
Results may differ from a plain program's by a relative error of at most 0.0029.
Values may be sent and summed in bfloat16 or wider, within the bound.
No kernel may reach another device: no remote copies, remote signals or barrier semaphores. Data moves between devices by JAX's collectives and lax.ppermute only.
A program may use at most 128 MiB of HBM per device.

v0:
```python
import jax
import jax.numpy as jnp
from jax import lax
from jax.sharding import PartitionSpec as P


def with_halo(value, sides, width):
    for axis, dim in sides:
        devices, length = (lax.axis_size(axis), value.shape[dim])
        up = [(i, (i + 1) % devices) for i in range(devices - 1)]
        down = [(j, i) for i, j in up]
        last = lax.slice_in_dim(value, length - width, length, axis=dim)
        leading = lax.slice_in_dim(value, 0, width, axis=dim)
        before = lax.ppermute(last, axis, up)
        after = lax.ppermute(leading, axis, down)
        value = jnp.concatenate([before, value, after], axis=dim)
    return value


def add_terms(total, padded, left_part, right_part, left_moves, right_moves, enabled_part):
    rows = total.shape[0]
    cols = total.shape[1]
    col_ids = jnp.arange(cols, dtype=jnp.int32)[None, :] + 1 + right_moves[:, None]

    def one_row(row_index):
        row_ids = row_index + 1 + left_moves
        picked = padded[row_ids[:, None], col_ids]
        inner = jnp.einsum(
            "wij,wcjk->wcik", left_part[row_index], picked, preferred_element_type=jnp.float32
        ).astype(jnp.bfloat16)
        inner = inner * jnp.transpose(enabled_part[row_index])[:, :, None, None]
        return jnp.einsum("wcik,cwdk->cid", inner, right_part, preferred_element_type=jnp.float32)

    return lax.map(one_row, jnp.arange(rows, dtype=jnp.int32))


def per_device(left_env, right_env, psi, left_shift, right_shift, active):
    padded = with_halo(psi, (("grp", 0), ("wide", 1)), 1)
    enabled = active.astype(jnp.bfloat16)
    start_total = jnp.zeros((psi.shape[0], psi.shape[1], psi.shape[2], psi.shape[3]), jnp.float32)
    left_all = lax.all_gather(left_env, "wide", axis=1, tiled=True)
    right_all = lax.all_gather(right_env, "grp", axis=1, tiled=True)
    return add_terms(start_total, padded, left_all, right_all, left_shift, right_shift, enabled)


def solution(mesh):
    return jax.shard_map(
        per_device,
        mesh=mesh,
        in_specs=(
            P("grp", "wide", None, None),
            P("wide", "grp", None, None),
            P("grp", "wide", None, None),
            P(),
            P(),
            P("grp", "wide", None),
        ),
        out_specs=P("grp", "wide", None, None),
        check_vma=False,
    )
```

profile of v0, /device:TPU:1, one launch (start us, length us, event | category | flops | bytes accessed | tf_op | source)
XLA Modules:
  0.0 459.8 jit_solution(1416285173617828692)
XLA Ops:
  6.5 0.7 all-gather.5.cloned.1.call-update
  7.3 0.7 all-gather.3.cloned.1.call-update
  8.0 1.1 fusion.35
  9.1 4.4 collective-permute-start
  13.5 1.3 collective-permute-start.1
  14.8 21.2 %collective-permute-done = bf16[1,8,128,128]{3,2,1,0:T(8,128)(2,1)S(1)} collective-permute-done((bf16[1,8,128,128]{3,2,1,0:T(8,128)(2,1)S(1)}, bf16[1,8,128,128]{3,2,1,0:T(8,128)(2,1)S(1)}, u32[]{:S(2)}, u32[]{:S(2)}) %collective-permute-start) | collective-permute-done | bytes 262176 | tf_op jit(solution)/shard_map/ppermute | solution.py:14
  36.0 0.3 constant_dynamic-update-slice_fusion.1
  36.3 1.5 copy-done
  37.9 8.6 %collective-permute-start.2 = (bf16[10,1,128,128]{3,2,1,0:T(8,128)(2,1)S(1)}, bf16[10,1,128,128]{3,2,1,0:T(8,128)(2,1)S(1)}, u32[]{:S(2)}, u32[]{:S(2)}) collective-permute-start(bf16[10,1,128,128]{3,2,1,0:T(8,128)(2,1)S(1)} %get-tuple-element.97), channel_id=1, source_target_pairs={{0,1},{1,2},{2,3},{3,4},{4,5},{5,6},{6,7},{7,8},{8,9},{9,10},{10,1... | collective-permute-start | bytes 983048 | tf_op jit(solution)/shard_map/ppermute | solution.py:14
  46.5 1.9 collective-permute-start.3
  48.5 18.1 %collective-permute-done.2 = bf16[10,1,128,128]{3,2,1,0:T(8,128)(2,1)S(1)} collective-permute-done((bf16[10,1,128,128]{3,2,1,0:T(8,128)(2,1)S(1)}, bf16[10,1,128,128]{3,2,1,0:T(8,128)(2,1)S(1)}, u32[]{:S(2)}, u32[]{:S(2)}) %collective-permute-start.2) | collective-permute-done | bytes 327712 | tf_op jit(solution)/shard_map/ppermute | solution.py:14
  66.6 0.7 copy-done.2
  67.4 3.9 collective-permute-done.3
  71.3 2.3 pad_maximum_fusion
  73.6 116.1 %all-gather.5.cloned.1.call-done = bf16[8,32,128,128]{3,2,1,0:T(8,128)(2,1)} async-done(((bf16[8,4,128,128]{3,2,1,0:T(8,128)(2,1)}), bf16[8,32,128,128]{3,2,1,0:T(8,128)(2,1)}) %all-gather.5.cloned.1.call-update) | async-done | bytes 8388624 | tf_op jit(solution)/shard_map/all_gather | solution.py:42
  189.6 84.0 %all-gather.3.cloned.1.call-done = bf16[8,32,128,128]{3,2,1,0:T(8,128)(2,1)} async-done(((bf16[8,2,128,128]{3,2,1,0:T(8,128)(2,1)}), bf16[8,32,128,128]{3,2,1,0:T(8,128)(2,1)}) %all-gather.3.cloned.1.call-update) | async-done | bytes 8388624 | tf_op jit(solution)/shard_map/all_gather | solution.py:41
  273.6 179.3 %while.11 = (s32[]{:T(128)}, f32[8,8,128,128]{3,2,1,0:T(8,128)}, s32[8]{0:T(128)S(1)}, s32[32]{0:T(128)S(1)}, bf16[10,10,128,128]{3,2,1,0:T(8,128)(2,1)S(1)}, /*...) while((s32[]{:T(128)}, f32[8,8,128,128]{3,2,1,0:T(8,128)}, ...), condition=%wide.region_1.2_spmd.clone, body=%wide.region_0.1_spmd.clone.sunk | while | flops 2155874304 | bytes 35137248 | solution.py:34
  273.6 0.6 dynamic_slice.24
  276.5 0.1 reshape.52
  276.6 10.0 %gather_fusion = bf16[256,128,128]{2,1,0:T(8,128)(2,1)} fusion(bf16[10,10,128,128]{3,2,1,0:T(8,128)(2,1)S(1)} %get-tuple-element.192, s32[256]{0:T(256)S(1)} %reshape.52), kind=kCustom, calls=%fused_computation.clone.clone.1 | custom fusion | bytes 16779264 | tf_op jit(solution)/shard_map/while/body/eval_jaxpr/gather | solution.py:27
  286.6 9.4 %fusion.50 = f32[8,8,128,128]{3,2,1,0:T(8,128)} fusion(f32[8,8,128,128]{3,2,1,0:T(8,128)} %get-tuple-element.176, s32[]{:T(128)} %get-tuple-element.175, bf16[8,32,128,128]{3,2,1,0:T(8,128)(2,1)} %get-tuple-element.195, bf16[32,8,128,128]{3,2,1,0:T(8,128)(2,1)} %bitcast.45, bf16[32,8]{0,1:T(8,128)(2,1)S(1)} %dynamic-slice_bitcast_fusion.2, ...), kind=kOutput, calls=%fused_computation.10.clone.1 | convolution fusion | flops 2155872256 | bytes 18351108 | tf_op jit(solution)/shard_map/while/body/eval_jaxpr/wcik,cwdk->cid/dot_general | solution.py:32
  296.0 0.6 dynamic_slice.24
  299.0 0.1 reshape.52
  299.0 10.0 %gather_fusion = bf16[256,128,128]{2,1,0:T(8,128)(2,1)} fusion(bf16[10,10,128,128]{3,2,1,0:T(8,128)(2,1)S(1)} %get-tuple-element.192, s32[256]{0:T(256)S(1)} %reshape.52), kind=kCustom, calls=%fused_computation.clone.clone.1 | custom fusion | bytes 16779264 | tf_op jit(solution)/shard_map/while/body/eval_jaxpr/gather | solution.py:27
  309.0 9.4 %fusion.50 = f32[8,8,128,128]{3,2,1,0:T(8,128)} fusion(f32[8,8,128,128]{3,2,1,0:T(8,128)} %get-tuple-element.176, s32[]{:T(128)} %get-tuple-element.175, bf16[8,32,128,128]{3,2,1,0:T(8,128)(2,1)} %get-tuple-element.195, bf16[32,8,128,128]{3,2,1,0:T(8,128)(2,1)} %bitcast.45, bf16[32,8]{0,1:T(8,128)(2,1)S(1)} %dynamic-slice_bitcast_fusion.2, ...), kind=kOutput, calls=%fused_computation.10.clone.1 | convolution fusion | flops 2155872256 | bytes 18351108 | tf_op jit(solution)/shard_map/while/body/eval_jaxpr/wcik,cwdk->cid/dot_general | solution.py:32
  318.4 0.6 dynamic_slice.24
  321.4 0.1 reshape.52
  321.5 10.0 %gather_fusion = bf16[256,128,128]{2,1,0:T(8,128)(2,1)} fusion(bf16[10,10,128,128]{3,2,1,0:T(8,128)(2,1)S(1)} %get-tuple-element.192, s32[256]{0:T(256)S(1)} %reshape.52), kind=kCustom, calls=%fused_computation.clone.clone.1 | custom fusion | bytes 16779264 | tf_op jit(solution)/shard_map/while/body/eval_jaxpr/gather | solution.py:27
  331.5 9.4 %fusion.50 = f32[8,8,128,128]{3,2,1,0:T(8,128)} fusion(f32[8,8,128,128]{3,2,1,0:T(8,128)} %get-tuple-element.176, s32[]{:T(128)} %get-tuple-element.175, bf16[8,32,128,128]{3,2,1,0:T(8,128)(2,1)} %get-tuple-element.195, bf16[32,8,128,128]{3,2,1,0:T(8,128)(2,1)} %bitcast.45, bf16[32,8]{0,1:T(8,128)(2,1)S(1)} %dynamic-slice_bitcast_fusion.2, ...), kind=kOutput, calls=%fused_computation.10.clone.1 | convolution fusion | flops 2155872256 | bytes 18351108 | tf_op jit(solution)/shard_map/while/body/eval_jaxpr/wcik,cwdk->cid/dot_general | solution.py:32
  340.9 0.6 dynamic_slice.24
  343.8 0.1 reshape.52
  343.9 10.0 %gather_fusion = bf16[256,128,128]{2,1,0:T(8,128)(2,1)} fusion(bf16[10,10,128,128]{3,2,1,0:T(8,128)(2,1)S(1)} %get-tuple-element.192, s32[256]{0:T(256)S(1)} %reshape.52), kind=kCustom, calls=%fused_computation.clone.clone.1 | custom fusion | bytes 16779264 | tf_op jit(solution)/shard_map/while/body/eval_jaxpr/gather | solution.py:27
  353.9 9.4 %fusion.50 = f32[8,8,128,128]{3,2,1,0:T(8,128)} fusion(f32[8,8,128,128]{3,2,1,0:T(8,128)} %get-tuple-element.176, s32[]{:T(128)} %get-tuple-element.175, bf16[8,32,128,128]{3,2,1,0:T(8,128)(2,1)} %get-tuple-element.195, bf16[32,8,128,128]{3,2,1,0:T(8,128)(2,1)} %bitcast.45, bf16[32,8]{0,1:T(8,128)(2,1)S(1)} %dynamic-slice_bitcast_fusion.2, ...), kind=kOutput, calls=%fused_computation.10.clone.1 | convolution fusion | flops 2155872256 | bytes 18351108 | tf_op jit(solution)/shard_map/while/body/eval_jaxpr/wcik,cwdk->cid/dot_general | solution.py:32
  363.3 0.6 dynamic_slice.24
  366.2 0.1 reshape.52
  366.3 10.0 %gather_fusion = bf16[256,128,128]{2,1,0:T(8,128)(2,1)} fusion(bf16[10,10,128,128]{3,2,1,0:T(8,128)(2,1)S(1)} %get-tuple-element.192, s32[256]{0:T(256)S(1)} %reshape.52), kind=kCustom, calls=%fused_computation.clone.clone.1 | custom fusion | bytes 16779264 | tf_op jit(solution)/shard_map/while/body/eval_jaxpr/gather | solution.py:27
  376.3 9.4 %fusion.50 = f32[8,8,128,128]{3,2,1,0:T(8,128)} fusion(f32[8,8,128,128]{3,2,1,0:T(8,128)} %get-tuple-element.176, s32[]{:T(128)} %get-tuple-element.175, bf16[8,32,128,128]{3,2,1,0:T(8,128)(2,1)} %get-tuple-element.195, bf16[32,8,128,128]{3,2,1,0:T(8,128)(2,1)} %bitcast.45, bf16[32,8]{0,1:T(8,128)(2,1)S(1)} %dynamic-slice_bitcast_fusion.2, ...), kind=kOutput, calls=%fused_computation.10.clone.1 | convolution fusion | flops 2155872256 | bytes 18351108 | tf_op jit(solution)/shard_map/while/body/eval_jaxpr/wcik,cwdk->cid/dot_general | solution.py:32
  385.7 0.6 dynamic_slice.24
  388.6 0.1 reshape.52
  388.7 10.0 %gather_fusion = bf16[256,128,128]{2,1,0:T(8,128)(2,1)} fusion(bf16[10,10,128,128]{3,2,1,0:T(8,128)(2,1)S(1)} %get-tuple-element.192, s32[256]{0:T(256)S(1)} %reshape.52), kind=kCustom, calls=%fused_computation.clone.clone.1 | custom fusion | bytes 16779264 | tf_op jit(solution)/shard_map/while/body/eval_jaxpr/gather | solution.py:27
  398.7 9.4 %fusion.50 = f32[8,8,128,128]{3,2,1,0:T(8,128)} fusion(f32[8,8,128,128]{3,2,1,0:T(8,128)} %get-tuple-element.176, s32[]{:T(128)} %get-tuple-element.175, bf16[8,32,128,128]{3,2,1,0:T(8,128)(2,1)} %get-tuple-element.195, bf16[32,8,128,128]{3,2,1,0:T(8,128)(2,1)} %bitcast.45, bf16[32,8]{0,1:T(8,128)(2,1)S(1)} %dynamic-slice_bitcast_fusion.2, ...), kind=kOutput, calls=%fused_computation.10.clone.1 | convolution fusion | flops 2155872256 | bytes 18351108 | tf_op jit(solution)/shard_map/while/body/eval_jaxpr/wcik,cwdk->cid/dot_general | solution.py:32
  408.1 0.6 dynamic_slice.24
  411.0 0.1 reshape.52
  411.1 10.0 %gather_fusion = bf16[256,128,128]{2,1,0:T(8,128)(2,1)} fusion(bf16[10,10,128,128]{3,2,1,0:T(8,128)(2,1)S(1)} %get-tuple-element.192, s32[256]{0:T(256)S(1)} %reshape.52), kind=kCustom, calls=%fused_computation.clone.clone.1 | custom fusion | bytes 16779264 | tf_op jit(solution)/shard_map/while/body/eval_jaxpr/gather | solution.py:27
  421.1 9.4 %fusion.50 = f32[8,8,128,128]{3,2,1,0:T(8,128)} fusion(f32[8,8,128,128]{3,2,1,0:T(8,128)} %get-tuple-element.176, s32[]{:T(128)} %get-tuple-element.175, bf16[8,32,128,128]{3,2,1,0:T(8,128)(2,1)} %get-tuple-element.195, bf16[32,8,128,128]{3,2,1,0:T(8,128)(2,1)} %bitcast.45, bf16[32,8]{0,1:T(8,128)(2,1)S(1)} %dynamic-slice_bitcast_fusion.2, ...), kind=kOutput, calls=%fused_computation.10.clone.1 | convolution fusion | flops 2155872256 | bytes 18351108 | tf_op jit(solution)/shard_map/while/body/eval_jaxpr/wcik,cwdk->cid/dot_general | solution.py:32
  430.5 0.6 dynamic_slice.24
  433.5 10.0 %gather_fusion = bf16[256,128,128]{2,1,0:T(8,128)(2,1)} fusion(bf16[10,10,128,128]{3,2,1,0:T(8,128)(2,1)S(1)} %get-tuple-element.192, s32[256]{0:T(256)S(1)} %reshape.52), kind=kCustom, calls=%fused_computation.clone.clone.1 | custom fusion | bytes 16779264 | tf_op jit(solution)/shard_map/while/body/eval_jaxpr/gather | solution.py:27
  443.5 9.4 %fusion.50 = f32[8,8,128,128]{3,2,1,0:T(8,128)} fusion(f32[8,8,128,128]{3,2,1,0:T(8,128)} %get-tuple-element.176, s32[]{:T(128)} %get-tuple-element.175, bf16[8,32,128,128]{3,2,1,0:T(8,128)(2,1)} %get-tuple-element.195, bf16[32,8,128,128]{3,2,1,0:T(8,128)(2,1)} %bitcast.45, bf16[32,8]{0,1:T(8,128)(2,1)S(1)} %dynamic-slice_bitcast_fusion.2, ...), kind=kOutput, calls=%fused_computation.10.clone.1 | convolution fusion | flops 2155872256 | bytes 18351108 | tf_op jit(solution)/shard_map/while/body/eval_jaxpr/wcik,cwdk->cid/dot_general | solution.py:32
  (53 shorter events, 1.6 us)
Async XLA Ops:
  6.5 29.4 %copy-start.1 = (bf16[8,8,128,128]{3,2,1,0:T(8,128)(2,1)S(1)}, bf16[8,8,128,128]{3,2,1,0:T(8,128)(2,1)}, u32[]{:S(2)}) copy-start(bf16[8,8,128,128]{3,2,1,0:T(8,128)(2,1)} %param.10) | copy-start | bytes 6291460
  6.5 183.1 %all-gather.5.cloned.1.call-start = ((), (), s32[]{:S(2)}) async-start(), calls=%async_computation.1 | async-start | bytes 9437184 | tf_op jit(solution)/shard_map/all_gather | solution.py:42
  7.3 41.2 %copy-start.3 = (s32[8,8,32]{2,1,0:T(8,128)S(1)}, s32[8,8,32]{2,1,0:T(8,128)}, u32[]{:S(2)}) copy-start(s32[8,8,32]{2,1,0:T(8,128)} %param.13) | copy-start | bytes 24580
  7.3 266.3 %all-gather.3.cloned.1.call-start = ((), (), s32[]{:S(2)}) async-start(), calls=%async_computation | async-start | bytes 8912896 | tf_op jit(solution)/shard_map/all_gather | solution.py:41
  9.1 26.9 %collective-permute-start = (bf16[1,8,128,128]{3,2,1,0:T(8,128)(2,1)S(1)}, bf16[1,8,128,128]{3,2,1,0:T(8,128)(2,1)S(1)}, u32[]{:S(2)}, u32[]{:S(2)}) collective-permute-start(bf16[1,8,128,128]{3,2,1,0:T(8,128)(2,1)S(1)} %get-tuple-element.100), channel_id=1, source_target_pairs={{0,16},{16,32},{32,48},{48,64},{64,80},{80,96},{96,112},{1,17},{17... | collective-permute-start | bytes 786440 | tf_op jit(solution)/shard_map/ppermute | solution.py:14
  13.5 22.8 %collective-permute-start.1 = (bf16[1,8,128,128]{3,2,1,0:T(8,128)(2,1)S(1)}, bf16[1,8,128,128]{3,2,1,0:T(8,128)(2,1)S(1)}, u32[]{:S(2)}, u32[]{:S(2)}) collective-permute-start(bf16[1,8,128,128]{3,2,1,0:T(8,128)(2,1)S(1)} %get-tuple-element.99), channel_id=1, source_target_pairs={{16,0},{32,16},{48,32},{64,48},{80,64},{96,80},{112,96},{17,1},{33... | collective-permute-start | bytes 786440 | tf_op jit(solution)/shard_map/ppermute | solution.py:15
  36.3 237.3 %copy-start.4 = (s32[32]{0:T(128)S(1)}, s32[32]{0:T(128)}, u32[]{:S(2)}) copy-start(s32[32]{0:T(128)} %param.12) | copy-start | bytes 388
  36.3 237.3 %copy-start.5 = (s32[32]{0:T(128)S(1)}, s32[32]{0:T(128)}, u32[]{:S(2)}) copy-start(s32[32]{0:T(128)} %param.11) | copy-start | bytes 388
  36.3 1.5 copy-start
  37.9 28.8 %collective-permute-start.2 = (bf16[10,1,128,128]{3,2,1,0:T(8,128)(2,1)S(1)}, bf16[10,1,128,128]{3,2,1,0:T(8,128)(2,1)S(1)}, u32[]{:S(2)}, u32[]{:S(2)}) collective-permute-start(bf16[10,1,128,128]{3,2,1,0:T(8,128)(2,1)S(1)} %get-tuple-element.97), channel_id=1, source_target_pairs={{0,1},{1,2},{2,3},{3,4},{4,5},{5,6},{6,7},{7,8},{8,9},{9,10},{10,1... | collective-permute-start | bytes 983048 | tf_op jit(solution)/shard_map/ppermute | solution.py:14
  46.5 24.8 %collective-permute-start.3 = (bf16[10,1,128,128]{3,2,1,0:T(8,128)(2,1)S(1)}, bf16[10,1,128,128]{3,2,1,0:T(8,128)(2,1)}, u32[]{:S(2)}, u32[]{:S(2)}) collective-permute-start(bf16[10,1,128,128]{3,2,1,0:T(8,128)(2,1)S(1)} %get-tuple-element.98), channel_id=1, source_target_pairs={{1,0},{2,1},{3,2},{4,3},{5,4},{6,5},{7,6},{8,7},{9,8},{10,9},{11,1... | collective-permute-start | bytes 983048 | tf_op jit(solution)/shard_map/ppermute | solution.py:15
  66.6 0.7 copy-start.2
Sparse Core Ops, SparseCore 0:
  9.0 180.5 all-gather.4
  192.1 81.4 all-gather.2
where the time goes:
time: 460 us
  waiting for transfers between devices  245 us (53%)
  local copies, waits for them, and re-layouts  89.4 us (19%)
  matrix products  75.2 us (16%)
  loops' own time  17.7 us (4%)
  starting transfers between devices  16.3 us (4%)
  between operations  13.5 us (3%)
    all_gather x1, waiting for transfers between devices, per_device(): right_all = lax.all_gather(right_env, 'grp', axis=1, tiled=True)  116 us
    all_gather x1, waiting for transfers between devices, per_device(): left_all = lax.all_gather(left_env, 'wide', axis=1, tiled=True)  84 us
    gather x8, local copies, waits for them, and re-layouts, one_row(): picked = padded[row_ids[:, None], col_ids]  79.9 us
    dot_general x8, matrix products, one_row(): jnp.einsum('wcik,cwdk->cid', inner, right_part, preferred_element_type=jn...  75.2 us
    ppermute x2, waiting for transfers between devices, with_halo(): before = lax.ppermute(last, axis, up)  39.3 us
    another operation x1, loops' own time, add_terms(): return lax.map(one_row, jnp.arange(rows, dtype=jnp.int32))  17.7 us
    ppermute x2, starting transfers between devices, with_halo(): before = lax.ppermute(last, axis, up)  13 us
  transfers between devices with their start and end apart: 6, of which 5 were waited for; matrix products, arithmetic and copies ran while one was open for 1% of the time, Pallas kernels for 0%

commit v1 on v0

--- a/solution.py
+++ b/solution.py
@@ -39,7 +39,9 @@
     enabled = active.astype(jnp.bfloat16)
     start_total = jnp.zeros((psi.shape[0], psi.shape[1], psi.shape[2], psi.shape[3]), jnp.float32)
     left_all = lax.all_gather(left_env, "wide", axis=1, tiled=True)
-    right_all = lax.all_gather(right_env, "grp", axis=1, tiled=True)
+    right_all = jnp.concatenate(
+        lax.all_to_all(jnp.stack([right_env] * lax.axis_size("grp")), "grp", 0, 0), axis=1
+    )
     return add_terms(start_total, padded, left_all, right_all, left_shift, right_shift, enabled)
 
 

time: 460 us -> 373 us (0.81)
  waiting for transfers between devices: 245 us -> 123 us
  local copies, waits for them, and re-layouts: 89.4 us -> 106 us
  matrix products: 75.2 us -> 82.6 us
  starting transfers between devices: 16.3 us -> 22.7 us
    all_gather x1 -> x0, waiting for transfers between devices: 116 us -> none  [per_device(): right_all = lax.all_gather(right_env, 'grp', axis=1, tiled=True)]
    all_gather x1, waiting for transfers between devices: 84 us -> 3.86 us  [per_device(): left_all = lax.all_gather(left_env, 'wide', axis=1, tiled=True)]
    ppermute x2, waiting for transfers between devices: 39.3 us -> 116 us  [with_halo(): before = lax.ppermute(last, axis, up)]
    all_to_all x0 -> x1, local copies, waits for them, and re-layouts: none -> 10.4 us  [per_device(): lax.all_to_all(jnp.stack([right_env] * lax.axis_size('grp')), 'grp', 0, 0)]
    dot_general x8, matrix products: 75.2 us -> 82.6 us  [one_row(): jnp.einsum('wcik,cwdk->cid', inner, right_part, preferred_element_type=jn...]
    another operation x0 -> x1, local copies, waits for them, and re-layouts: none -> 6.61 us  [per_device(): jnp.stack([right_env] * lax.axis_size('grp'))]
    all_to_all x0 -> x1, starting transfers between devices: none -> 6.33 us  [per_device(): lax.all_to_all(jnp.stack([right_env] * lax.axis_size('grp')), 'grp', 0, 0)]
  transfers between devices with their start and end apart: 6 -> 6, of which waited for: 5 -> 4; matrix products, arithmetic and copies ran while one was open for 1% -> 5% of each run, Pallas kernels for 0% -> 0%
where the time goes in v1:
time: 373 us
  waiting for transfers between devices  123 us (33%)
  local copies, waits for them, and re-layouts  106 us (28%)
  matrix products  82.6 us (22%)
  starting transfers between devices  22.7 us (6%)
  loops' own time  21.8 us (6%)
  between operations  13.5 us (4%)
    ppermute x2, waiting for transfers between devices, with_halo(): before = lax.ppermute(last, axis, up)  116 us
    dot_general x8, matrix products, one_row(): jnp.einsum('wcik,cwdk->cid', inner, right_part, preferred_element_type=jn...  82.6 us
    gather x8, local copies, waits for them, and re-layouts, one_row(): picked = padded[row_ids[:, None], col_ids]  79.9 us
    another operation x1, loops' own time, add_terms(): return lax.map(one_row, jnp.arange(rows, dtype=jnp.int32))  21.8 us
    ppermute x2, starting transfers between devices, with_halo(): before = lax.ppermute(last, axis, up)  13.2 us
    all_to_all x1, local copies, waits for them, and re-layouts, per_device(): lax.all_to_all(jnp.stack([right_env] * lax.axis_size('grp')), 'grp', 0, 0)  10.4 us
  transfers between devices with their start and end apart: 6, of which 4 were waited for; matrix products, arithmetic and copies ran while one was open for 5% of the time, Pallas kernels for 0%

profile of v1, /device:TPU:1, one launch (start us, length us, event | category | flops | bytes accessed | tf_op | source)
XLA Modules:
  0.0 372.7 jit_solution(14686473570701526023)
XLA Ops:
  6.5 0.7 all-gather.2.cloned.1.call-update
  7.3 6.6 %stack.2 = bf16[8,8,4,128,128]{4,3,2,1,0:T(8,128)(2,1)} broadcast(bf16[8,4,128,128]{3,2,1,0:T(8,128)(2,1)} %param.9), dimensions={1,2,3,4} | broadcast | bytes 9437184 | tf_op jit(solution)/shard_map/stack | solution.py:43
  13.9 6.3 %all-to-all-start = ((bf16[8,8,4,128,128]{4,3,2,1,0:T(8,128)(2,1)}), bf16[8,8,4,128,128]{4,3,2,1,0:T(8,128)(2,1)}, u32[]{:S(2)}, u32[]{:S(2)}) async-start(bf16[8,8,4,128,128]{4,3,2,1,0:T(8,128)(2,1)} %stack.2), calls=%async_computation | async-start | bytes 16777216 | tf_op jit(solution)/shard_map/all_to_all | solution.py:43
  20.3 3.4 collective-permute-start
  23.6 1.3 collective-permute-start.1
  24.9 103.7 %collective-permute-done = bf16[1,8,128,128]{3,2,1,0:T(8,128)(2,1)S(1)} collective-permute-done((bf16[1,8,128,128]{3,2,1,0:T(8,128)(2,1)S(1)}, bf16[1,8,128,128]{3,2,1,0:T(8,128)(2,1)S(1)}, u32[]{:S(2)}, u32[]{:S(2)}) %collective-permute-start) | collective-permute-done | bytes 262176 | tf_op jit(solution)/shard_map/ppermute | solution.py:14
  128.6 0.3 constant_dynamic-update-slice_fusion.1
  128.9 2.9 collective-permute-done.1
  131.9 1.5 copy-done
  133.5 9.8 %collective-permute-start.2 = (bf16[10,1,128,128]{3,2,1,0:T(8,128)(2,1)S(1)}, bf16[10,1,128,128]{3,2,1,0:T(8,128)(2,1)S(1)}, u32[]{:S(2)}, u32[]{:S(2)}) collective-permute-start(bf16[10,1,128,128]{3,2,1,0:T(8,128)(2,1)S(1)} %get-tuple-element.97), channel_id=1, source_target_pairs={{0,1},{1,2},{2,3},{3,4},{4,5},{5,6},{6,7},{7,8},{8,9},{9,10},{10,1... | collective-permute-start | bytes 983048 | tf_op jit(solution)/shard_map/ppermute | solution.py:14
  143.3 1.9 collective-permute-start.3
  145.2 11.9 %collective-permute-done.2 = bf16[10,1,128,128]{3,2,1,0:T(8,128)(2,1)S(1)} collective-permute-done((bf16[10,1,128,128]{3,2,1,0:T(8,128)(2,1)S(1)}, bf16[10,1,128,128]{3,2,1,0:T(8,128)(2,1)S(1)}, u32[]{:S(2)}, u32[]{:S(2)}) %collective-permute-start.2) | collective-permute-done | bytes 327712 | tf_op jit(solution)/shard_map/ppermute | solution.py:14
  157.2 0.7 copy-done.2
  157.9 2.3 pad_maximum_fusion
  160.2 10.4 %copy.14 = bf16[8,8,4,128,128]{4,3,2,0,1:T(8,128)(2,1)} copy(bf16[8,8,4,128,128]{4,3,2,1,0:T(8,128)(2,1)} %all-to-all-done) | data formatting | bytes 16777216 | tf_op jit(solution)/shard_map/all_to_all | solution.py:43
  170.5 3.9 %all-gather.2.cloned.1.call-done = bf16[8,32,128,128]{3,2,1,0:T(8,128)(2,1)} async-done(((bf16[8,2,128,128]{3,2,1,0:T(8,128)(2,1)}), bf16[8,32,128,128]{3,2,1,0:T(8,128)(2,1)}) %all-gather.2.cloned.1.call-update) | async-done | bytes 8388624 | tf_op jit(solution)/shard_map/all_gather | solution.py:41
  174.4 191.5 %while.11 = (s32[]{:T(128)}, f32[8,8,128,128]{3,2,1,0:T(8,128)}, s32[8]{0:T(128)S(1)}, s32[32]{0:T(128)S(1)}, bf16[10,10,128,128]{3,2,1,0:T(8,128)(2,1)S(1)}, /*...) while((s32[]{:T(128)}, f32[8,8,128,128]{3,2,1,0:T(8,128)}, ...), condition=%wide.region_1.2_spmd.clone, body=%wide.region_0.1_spmd.clone.sunk | while | flops 2155874304 | bytes 35137248 | solution.py:34
  174.4 0.6 dynamic_slice.24
  177.9 0.1 reshape.62
  178.0 10.0 %gather_fusion = bf16[256,128,128]{2,1,0:T(8,128)(2,1)} fusion(bf16[10,10,128,128]{3,2,1,0:T(8,128)(2,1)S(1)} %get-tuple-element.192, s32[256]{0:T(256)S(1)} %reshape.62), kind=kCustom, calls=%fused_computation.clone.clone.1 | custom fusion | bytes 16779264 | tf_op jit(solution)/shard_map/while/body/eval_jaxpr/gather | solution.py:27
  188.0 10.3 %fusion.50 = f32[8,8,128,128]{3,2,1,0:T(8,128)} fusion(f32[8,8,128,128]{3,2,1,0:T(8,128)} %get-tuple-element.176, s32[]{:T(128)} %get-tuple-element.175, bf16[8,32,128,128]{3,2,1,0:T(8,128)(2,1)} %get-tuple-element.195, bf16[32,8,128,128]{3,2,1,0:T(8,128)(2,1)} %bitcast.48, bf16[32,8]{0,1:T(8,128)(2,1)S(1)} %dynamic-slice_bitcast_fusion.2, ...), kind=kOutput, calls=%fused_computation.10.clone.1 | convolution fusion | flops 2155872256 | bytes 18351108 | tf_op jit(solution)/shard_map/while/body/eval_jaxpr/wcik,cwdk->cid/dot_general | solution.py:32
  198.3 0.6 dynamic_slice.24
  201.9 0.1 reshape.62
  202.0 10.0 %gather_fusion = bf16[256,128,128]{2,1,0:T(8,128)(2,1)} fusion(bf16[10,10,128,128]{3,2,1,0:T(8,128)(2,1)S(1)} %get-tuple-element.192, s32[256]{0:T(256)S(1)} %reshape.62), kind=kCustom, calls=%fused_computation.clone.clone.1 | custom fusion | bytes 16779264 | tf_op jit(solution)/shard_map/while/body/eval_jaxpr/gather | solution.py:27
  211.9 10.3 %fusion.50 = f32[8,8,128,128]{3,2,1,0:T(8,128)} fusion(f32[8,8,128,128]{3,2,1,0:T(8,128)} %get-tuple-element.176, s32[]{:T(128)} %get-tuple-element.175, bf16[8,32,128,128]{3,2,1,0:T(8,128)(2,1)} %get-tuple-element.195, bf16[32,8,128,128]{3,2,1,0:T(8,128)(2,1)} %bitcast.48, bf16[32,8]{0,1:T(8,128)(2,1)S(1)} %dynamic-slice_bitcast_fusion.2, ...), kind=kOutput, calls=%fused_computation.10.clone.1 | convolution fusion | flops 2155872256 | bytes 18351108 | tf_op jit(solution)/shard_map/while/body/eval_jaxpr/wcik,cwdk->cid/dot_general | solution.py:32
  222.3 0.6 dynamic_slice.24
  225.8 0.1 reshape.62
  225.9 10.0 %gather_fusion = bf16[256,128,128]{2,1,0:T(8,128)(2,1)} fusion(bf16[10,10,128,128]{3,2,1,0:T(8,128)(2,1)S(1)} %get-tuple-element.192, s32[256]{0:T(256)S(1)} %reshape.62), kind=kCustom, calls=%fused_computation.clone.clone.1 | custom fusion | bytes 16779264 | tf_op jit(solution)/shard_map/while/body/eval_jaxpr/gather | solution.py:27
  235.9 10.3 %fusion.50 = f32[8,8,128,128]{3,2,1,0:T(8,128)} fusion(f32[8,8,128,128]{3,2,1,0:T(8,128)} %get-tuple-element.176, s32[]{:T(128)} %get-tuple-element.175, bf16[8,32,128,128]{3,2,1,0:T(8,128)(2,1)} %get-tuple-element.195, bf16[32,8,128,128]{3,2,1,0:T(8,128)(2,1)} %bitcast.48, bf16[32,8]{0,1:T(8,128)(2,1)S(1)} %dynamic-slice_bitcast_fusion.2, ...), kind=kOutput, calls=%fused_computation.10.clone.1 | convolution fusion | flops 2155872256 | bytes 18351108 | tf_op jit(solution)/shard_map/while/body/eval_jaxpr/wcik,cwdk->cid/dot_general | solution.py:32
  246.2 0.6 dynamic_slice.24
  249.8 0.1 reshape.62
  249.8 10.0 %gather_fusion = bf16[256,128,128]{2,1,0:T(8,128)(2,1)} fusion(bf16[10,10,128,128]{3,2,1,0:T(8,128)(2,1)S(1)} %get-tuple-element.192, s32[256]{0:T(256)S(1)} %reshape.62), kind=kCustom, calls=%fused_computation.clone.clone.1 | custom fusion | bytes 16779264 | tf_op jit(solution)/shard_map/while/body/eval_jaxpr/gather | solution.py:27
  259.8 10.3 %fusion.50 = f32[8,8,128,128]{3,2,1,0:T(8,128)} fusion(f32[8,8,128,128]{3,2,1,0:T(8,128)} %get-tuple-element.176, s32[]{:T(128)} %get-tuple-element.175, bf16[8,32,128,128]{3,2,1,0:T(8,128)(2,1)} %get-tuple-element.195, bf16[32,8,128,128]{3,2,1,0:T(8,128)(2,1)} %bitcast.48, bf16[32,8]{0,1:T(8,128)(2,1)S(1)} %dynamic-slice_bitcast_fusion.2, ...), kind=kOutput, calls=%fused_computation.10.clone.1 | convolution fusion | flops 2155872256 | bytes 18351108 | tf_op jit(solution)/shard_map/while/body/eval_jaxpr/wcik,cwdk->cid/dot_general | solution.py:32
  270.1 0.6 dynamic_slice.24
  273.7 0.1 reshape.62
  273.8 10.0 %gather_fusion = bf16[256,128,128]{2,1,0:T(8,128)(2,1)} fusion(bf16[10,10,128,128]{3,2,1,0:T(8,128)(2,1)S(1)} %get-tuple-element.192, s32[256]{0:T(256)S(1)} %reshape.62), kind=kCustom, calls=%fused_computation.clone.clone.1 | custom fusion | bytes 16779264 | tf_op jit(solution)/shard_map/while/body/eval_jaxpr/gather | solution.py:27
  283.8 10.3 %fusion.50 = f32[8,8,128,128]{3,2,1,0:T(8,128)} fusion(f32[8,8,128,128]{3,2,1,0:T(8,128)} %get-tuple-element.176, s32[]{:T(128)} %get-tuple-element.175, bf16[8,32,128,128]{3,2,1,0:T(8,128)(2,1)} %get-tuple-element.195, bf16[32,8,128,128]{3,2,1,0:T(8,128)(2,1)} %bitcast.48, bf16[32,8]{0,1:T(8,128)(2,1)S(1)} %dynamic-slice_bitcast_fusion.2, ...), kind=kOutput, calls=%fused_computation.10.clone.1 | convolution fusion | flops 2155872256 | bytes 18351108 | tf_op jit(solution)/shard_map/while/body/eval_jaxpr/wcik,cwdk->cid/dot_general | solution.py:32
  294.1 0.6 dynamic_slice.24
  297.6 0.1 reshape.62
  297.7 10.0 %gather_fusion = bf16[256,128,128]{2,1,0:T(8,128)(2,1)} fusion(bf16[10,10,128,128]{3,2,1,0:T(8,128)(2,1)S(1)} %get-tuple-element.192, s32[256]{0:T(256)S(1)} %reshape.62), kind=kCustom, calls=%fused_computation.clone.clone.1 | custom fusion | bytes 16779264 | tf_op jit(solution)/shard_map/while/body/eval_jaxpr/gather | solution.py:27
  307.7 10.3 %fusion.50 = f32[8,8,128,128]{3,2,1,0:T(8,128)} fusion(f32[8,8,128,128]{3,2,1,0:T(8,128)} %get-tuple-element.176, s32[]{:T(128)} %get-tuple-element.175, bf16[8,32,128,128]{3,2,1,0:T(8,128)(2,1)} %get-tuple-element.195, bf16[32,8,128,128]{3,2,1,0:T(8,128)(2,1)} %bitcast.48, bf16[32,8]{0,1:T(8,128)(2,1)S(1)} %dynamic-slice_bitcast_fusion.2, ...), kind=kOutput, calls=%fused_computation.10.clone.1 | convolution fusion | flops 2155872256 | bytes 18351108 | tf_op jit(solution)/shard_map/while/body/eval_jaxpr/wcik,cwdk->cid/dot_general | solution.py:32
  318.0 0.6 dynamic_slice.24
  321.6 0.1 reshape.62
  321.7 10.0 %gather_fusion = bf16[256,128,128]{2,1,0:T(8,128)(2,1)} fusion(bf16[10,10,128,128]{3,2,1,0:T(8,128)(2,1)S(1)} %get-tuple-element.192, s32[256]{0:T(256)S(1)} %reshape.62), kind=kCustom, calls=%fused_computation.clone.clone.1 | custom fusion | bytes 16779264 | tf_op jit(solution)/shard_map/while/body/eval_jaxpr/gather | solution.py:27
  331.6 10.3 %fusion.50 = f32[8,8,128,128]{3,2,1,0:T(8,128)} fusion(f32[8,8,128,128]{3,2,1,0:T(8,128)} %get-tuple-element.176, s32[]{:T(128)} %get-tuple-element.175, bf16[8,32,128,128]{3,2,1,0:T(8,128)(2,1)} %get-tuple-element.195, bf16[32,8,128,128]{3,2,1,0:T(8,128)(2,1)} %bitcast.48, bf16[32,8]{0,1:T(8,128)(2,1)S(1)} %dynamic-slice_bitcast_fusion.2, ...), kind=kOutput, calls=%fused_computation.10.clone.1 | convolution fusion | flops 2155872256 | bytes 18351108 | tf_op jit(solution)/shard_map/while/body/eval_jaxpr/wcik,cwdk->cid/dot_general | solution.py:32
  342.0 0.6 dynamic_slice.24
  345.6 10.0 %gather_fusion = bf16[256,128,128]{2,1,0:T(8,128)(2,1)} fusion(bf16[10,10,128,128]{3,2,1,0:T(8,128)(2,1)S(1)} %get-tuple-element.192, s32[256]{0:T(256)S(1)} %reshape.62), kind=kCustom, calls=%fused_computation.clone.clone.1 | custom fusion | bytes 16779264 | tf_op jit(solution)/shard_map/while/body/eval_jaxpr/gather | solution.py:27
  355.6 10.3 %fusion.50 = f32[8,8,128,128]{3,2,1,0:T(8,128)} fusion(f32[8,8,128,128]{3,2,1,0:T(8,128)} %get-tuple-element.176, s32[]{:T(128)} %get-tuple-element.175, bf16[8,32,128,128]{3,2,1,0:T(8,128)(2,1)} %get-tuple-element.195, bf16[32,8,128,128]{3,2,1,0:T(8,128)(2,1)} %bitcast.48, bf16[32,8]{0,1:T(8,128)(2,1)S(1)} %dynamic-slice_bitcast_fusion.2, ...), kind=kOutput, calls=%fused_computation.10.clone.1 | convolution fusion | flops 2155872256 | bytes 18351108 | tf_op jit(solution)/shard_map/while/body/eval_jaxpr/wcik,cwdk->cid/dot_general | solution.py:32
  (54 shorter events, 1.6 us)
Async XLA Ops:
  6.5 167.9 %all-gather.2.cloned.1.call-start = ((), (), s32[]{:S(2)}) async-start(), calls=%async_computation.1 | async-start | bytes 8912896 | tf_op jit(solution)/shard_map/all_gather | solution.py:41
  13.9 6.3 %copy-start.1 = (bf16[8,8,128,128]{3,2,1,0:T(8,128)(2,1)S(1)}, bf16[8,8,128,128]{3,2,1,0:T(8,128)(2,1)}, u32[]{:S(2)}) copy-start(bf16[8,8,128,128]{3,2,1,0:T(8,128)(2,1)} %param.10) | copy-start | bytes 6291460
  13.9 146.3 %all-to-all-start = ((bf16[8,8,4,128,128]{4,3,2,1,0:T(8,128)(2,1)}), bf16[8,8,4,128,128]{4,3,2,1,0:T(8,128)(2,1)}, u32[]{:S(2)}, u32[]{:S(2)}) async-start(bf16[8,8,4,128,128]{4,3,2,1,0:T(8,128)(2,1)} %stack.2), calls=%async_computation | async-start | bytes 16777216 | tf_op jit(solution)/shard_map/all_to_all | solution.py:43
  20.2 125.0 %copy-start.3 = (s32[8,8,32]{2,1,0:T(8,128)S(1)}, s32[8,8,32]{2,1,0:T(8,128)}, u32[]{:S(2)}) copy-start(s32[8,8,32]{2,1,0:T(8,128)} %param.13) | copy-start | bytes 24580
  20.3 108.3 %collective-permute-start = (bf16[1,8,128,128]{3,2,1,0:T(8,128)(2,1)S(1)}, bf16[1,8,128,128]{3,2,1,0:T(8,128)(2,1)S(1)}, u32[]{:S(2)}, u32[]{:S(2)}) collective-permute-start(bf16[1,8,128,128]{3,2,1,0:T(8,128)(2,1)S(1)} %get-tuple-element.100), channel_id=1, source_target_pairs={{0,16},{16,32},{32,48},{48,64},{64,80},{80,96},{96,112},{1,17},{17... | collective-permute-start | bytes 786440 | tf_op jit(solution)/shard_map/ppermute | solution.py:14
  23.6 108.2 %collective-permute-start.1 = (bf16[1,8,128,128]{3,2,1,0:T(8,128)(2,1)S(1)}, bf16[1,8,128,128]{3,2,1,0:T(8,128)(2,1)S(1)}, u32[]{:S(2)}, u32[]{:S(2)}) collective-permute-start(bf16[1,8,128,128]{3,2,1,0:T(8,128)(2,1)S(1)} %get-tuple-element.99), channel_id=1, source_target_pairs={{16,0},{32,16},{48,32},{64,48},{80,64},{96,80},{112,96},{17,1},{33... | collective-permute-start | bytes 786440 | tf_op jit(solution)/shard_map/ppermute | solution.py:15
  131.8 1.6 copy-start
  133.5 23.7 %collective-permute-start.2 = (bf16[10,1,128,128]{3,2,1,0:T(8,128)(2,1)S(1)}, bf16[10,1,128,128]{3,2,1,0:T(8,128)(2,1)S(1)}, u32[]{:S(2)}, u32[]{:S(2)}) collective-permute-start(bf16[10,1,128,128]{3,2,1,0:T(8,128)(2,1)S(1)} %get-tuple-element.97), channel_id=1, source_target_pairs={{0,1},{1,2},{2,3},{3,4},{4,5},{5,6},{6,7},{7,8},{8,9},{9,10},{10,1... | collective-permute-start | bytes 983048 | tf_op jit(solution)/shard_map/ppermute | solution.py:14
  143.3 14.6 %collective-permute-start.3 = (bf16[10,1,128,128]{3,2,1,0:T(8,128)(2,1)S(1)}, bf16[10,1,128,128]{3,2,1,0:T(8,128)(2,1)}, u32[]{:S(2)}, u32[]{:S(2)}) collective-permute-start(bf16[10,1,128,128]{3,2,1,0:T(8,128)(2,1)S(1)} %get-tuple-element.98), channel_id=1, source_target_pairs={{1,0},{2,1},{3,2},{4,3},{5,4},{6,5},{7,6},{8,7},{9,8},{10,9},{11,1... | collective-permute-start | bytes 983048 | tf_op jit(solution)/shard_map/ppermute | solution.py:15
  157.1 0.7 copy-start.2
  160.1 14.3 %copy-start.4 = (s32[32]{0:T(128)S(1)}, s32[32]{0:T(128)}, u32[]{:S(2)}) copy-start(s32[32]{0:T(128)} %param.12) | copy-start | bytes 388
  160.1 14.3 %copy-start.5 = (s32[32]{0:T(128)S(1)}, s32[32]{0:T(128)}, u32[]{:S(2)}) copy-start(s32[32]{0:T(128)} %param.11) | copy-start | bytes 388
Sparse Core Ops, SparseCore 0:
  9.8 164.5 all-gather.1
